TPU v7x, 256 devices: a whole 4x4x8 slice. The times are simulated.
256 devices in a mesh: row: 32 (over z, x), col: 4 (over y), rep: 2 (over core).
Axes of the slice: x: 4, y: 4, z: 8, core: 2. Of those that a mesh axis runs over, the one named last changes fastest.
Arguments:
- amplitudes: bfloat16 [32768, 8192], P('row', ('rep', 'col')), may hold values from -6 to 6
- integrals: bfloat16 [8192, 4096], P(('rep', 'row'), 'col'), may hold values from -0.1875 to 0.1875
- tile_mask: int32 [64, 32], replicated, may hold values from 0 to 1
- k_irrep: int32 [64], replicated, may hold values from 0 to 3
- n_irrep: int32 [32], replicated, may hold values from 0 to 3
- stored_tile: int32 [64], replicated, may hold values from 0 to 63, as said below
Outputs:
- ladder: bfloat16 [32768, 4096], P('row', ('col', 'rep'))
Inputs may be any that keep to these rules, and one draw needn't show every extreme that they name: `stored_tile`: for each q, slots q * 32 to (q + 1) * 32 - 1 hold a permutation of the tiles q * 32 to (q + 1) * 32 - 1.
All inputs are finite; a program needn't handle non-finite values.
Results may differ from a plain program's by a relative error of at most 0.001.
Values may be sent and summed in bfloat16 or wider, within the bound.
No kernel may reach another device: no remote copies, remote signals or barrier semaphores. Data moves between devices by JAX's collectives and lax.ppermute only.
A program may use at most 128 MiB of HBM per device.

v0:
```python
import jax
import jax.numpy as jnp
from jax import lax
from jax.sharding import PartitionSpec as P

TS = 128


def on_device(amplitudes, integrals, tile_mask, k_irrep, n_irrep, stored_tile):
    slab = lax.axis_index("rep")
    column = lax.axis_index("col")
    ncol = integrals.shape[1]
    tiles_col = ncol // TS
    n_labels = lax.dynamic_slice_in_dim(n_irrep, column * tiles_col, tiles_col)
    mask_cols = lax.dynamic_slice_in_dim(tile_mask, column * tiles_col, tiles_col, 1)
    stored_rows = integrals.shape[0]
    kq = stored_rows * lax.axis_size("row")
    slab_tiles = kq // TS
    slots = lax.dynamic_slice_in_dim(stored_tile, slab * slab_tiles, slab_tiles)
    gathered = lax.all_gather(integrals, "row", axis=0, tiled=True)
    same = jnp.take(k_irrep, slots)[:, None] == n_labels[None, :]
    occupied = jnp.take(mask_cols, slots, axis=0) == 1
    weights = jnp.logical_and(same, occupied).astype(jnp.bfloat16)
    shaped = gathered.reshape(slab_tiles, TS, tiles_col, TS) * weights[:, None, :, None]
    masked = shaped.reshape(kq, ncol)
    amp_slab = lax.all_gather(amplitudes, "col", axis=1, tiled=True)
    mrow = amp_slab.shape[0]
    local_ids = slots - slab * slab_tiles
    ordered = jnp.take(amp_slab.reshape(mrow, slab_tiles, TS), local_ids, axis=1).reshape(mrow, kq)
    partial_value = jnp.dot(ordered, masked, preferred_element_type=jnp.float32)
    return lax.psum_scatter(partial_value, "rep", scatter_dimension=1, tiled=True).astype(
        jnp.bfloat16
    )


def solution(mesh):
    placed = (P("row", ("rep", "col")), P(("rep", "row"), "col"), P(), P(), P(), P())
    return jax.shard_map(
        on_device, mesh=mesh, in_specs=placed, out_specs=P("row", ("col", "rep")), check_vma=False
    )
```

profile of v0, /device:TPU:1, one launch (start us, length us, event | category | flops | bytes accessed | tf_op | source)
XLA Modules:
  0.0 242.3 jit_solution(16062950526228524270)
XLA Ops:
  6.5 3.9 %copy.13 = bf16[1024,1024]{0,1:T(8,128)(2,1)} copy(bf16[1024,1024]{1,0:T(8,128)(2,1)} %param.6) | data formatting | bytes 4194304 | tf_op args[0]
  10.5 0.0 all-gather.5.cloned.1.call-start
  10.6 0.7 all-gather.5.cloned.1.call-update
  11.3 0.0 reduce-scatter.2.cloned.1.call-start
  11.3 0.7 dynamic_slice.10
  12.0 0.1 copy.19
  12.1 0.7 compare_and_fusion
  12.9 1.4 gather_fusion.1
  14.2 0.6 gather_fusion.2
  14.8 0.1 copy.17
  14.9 0.1 fusion.3
  15.0 0.1 copy.18
  15.1 0.1 broadcast_bitcast_fusion
  15.1 84.8 %all-gather.3.cloned.1.call-done = bf16[1024,4096]{0,1:T(8,128)(2,1)} async-done(((bf16[1024,1024]{0,1:T(8,128)(2,1)}), bf16[1024,4096]{0,1:T(8,128)(2,1)}) %all-gather.3.cloned.1.call-update) | async-done | bytes 8388624 | tf_op jit(solution)/shard_map/all_gather | solution.py:26
  99.9 12.0 %copy.14 = bf16[1024,32,128]{2,0,1:T(8,128)(2,1)} copy(bf16[1024,32,128]{0,2,1:T(8,128)(2,1)} %bitcast.14) | data formatting | bytes 16777216 | tf_op jit(solution)/shard_map/reshape | solution.py:29
  111.9 8.4 %gather_fusion = bf16[32,1024,128]{2,1,0:T(8,128)(2,1)} fusion(bf16[1024,32,128]{2,0,1:T(8,128)(2,1)} %copy.14, s32[1024]{0:T(1024)S(1)} %pad_clamp_fusion.1), kind=kCustom, calls=%fused_computation | custom fusion | bytes 16777344 | tf_op jit(solution)/shard_map/jit(_take)/gather | solution.py:29
  120.3 12.0 %copy.15 = bf16[1024,32,128]{0,2,1:T(8,128)(2,1)} copy(bf16[1024,32,128]{2,0,1:T(8,128)(2,1)} %bitcast.12) | data formatting | bytes 16777216 | tf_op jit(solution)/shard_map/jit(_take)/gather | solution.py:29
  132.3 7.3 %bitcast_select_fusion = bf16[1024,4096]{0,1:T(8,128)(2,1)} fusion(bf16[1024,32,128]{0,2,1:T(8,128)(2,1)} %copy.15, pred[4096]{0:T(1024)(128)(4,1)S(1)} %broadcast_bitcast_fusion), kind=kLoop, calls=%fused_computation.6 | loop fusion | flops 4194304 | bytes 16781312 | tf_op jit(solution)/shard_map/jit(_take)/select_n | solution.py:29
  139.6 61.2 %all-gather.5.cloned.1.call-done = bf16[4096,1024]{1,0:T(8,128)(2,1)} async-done(((bf16[128,1024]{1,0:T(8,128)(2,1)}), bf16[4096,1024]{1,0:T(8,128)(2,1)}) %all-gather.5.cloned.1.call-update) | async-done | bytes 8388624 | tf_op jit(solution)/shard_map/all_gather | solution.py:20
  200.8 1.1 mul.21
  201.9 2.2 copy-done.2
  204.2 13.0 %fusion = f32[1024,1024]{1,0:T(8,128)} fusion(bf16[1024,4096]{0,1:T(8,128)(2,1)S(1)} %copy-done.2, bf16[4096,1024]{1,0:T(8,128)(2,1)} %all-gather.5.cloned.1.call-done, bf16[512,8,8,128]{3,2,1,0:T(8,128)(2,1)S(1)} %bitcast.13), kind=kOutput, calls=%fused_computation.4 | convolution fusion | flops 8594128896 | bytes 29360128 | tf_op jit(solution)/shard_map/dot_general | solution.py:30
  217.1 16.0 %reduce-scatter.2.cloned.1.call-done = f32[1024,512]{1,0:T(8,128)} async-done(((f32[1024,1024]{1,0:T(8,128)}), f32[1024,512]{1,0:T(8,128)}) %reduce-scatter.2.cloned.1.call-update) | async-done | bytes 2097168 | tf_op jit(solution)/shard_map/reduce_scatter | solution.py:31
  233.1 2.7 %convert_element_type.11 = bf16[1024,512]{1,0:T(8,128)(2,1)} convert(f32[1024,512]{1,0:T(8,128)} %reduce-scatter.2.cloned.1.call-done) | non-fusion elementwise | flops 524288 | bytes 3145728 | tf_op jit(solution)/shard_map/convert_element_type | solution.py:31
  (12 shorter events, 0.1 us)
Async XLA Ops:
  6.5 5.5 %copy-start = (s32[64,32]{0,1:T(8,128)S(1)}, s32[64,32]{0,1:T(8,128)}, u32[]{:S(2)}) copy-start(s32[64,32]{0,1:T(8,128)} %param.8) | copy-start | bytes 24580
  6.5 93.4 %all-gather.3.cloned.1.call-start = ((), (), s32[]{:S(2)}) async-start(), calls=%async_computation.1 | async-start | bytes 10485760 | tf_op jit(solution)/shard_map/all_gather | solution.py:26
  10.5 190.3 %all-gather.5.cloned.1.call-start = ((), (), s32[]{:S(2)}) async-start(), calls=%async_computation.2 | async-start | bytes 8650752 | tf_op jit(solution)/shard_map/all_gather | solution.py:20
  11.3 221.9 %reduce-scatter.2.cloned.1.call-start = ((), (), s32[]{:S(2)}) async-start(), calls=%async_computation.3 | async-start | bytes 6291456 | tf_op jit(solution)/shard_map/reduce_scatter | solution.py:31
  200.8 3.4 %copy-start.2 = (bf16[1024,4096]{0,1:T(8,128)(2,1)S(1)}, bf16[1024,4096]{0,1:T(8,128)(2,1)}, u32[]{:S(2)}) copy-start(bf16[1024,4096]{0,1:T(8,128)(2,1)} %bitcast_select_fusion) | copy-start | bytes 25165828
  204.2 31.7 %copy-start.1 = (s32[64,32]{0,1:T(8,128)S(1)}, s32[64,32]{0,1:T(8,128)}, u32[]{:S(2)}) copy-start(s32[64,32]{0,1:T(8,128)} %param.8) | copy-start | bytes 24580
Sparse Core Ops, SparseCore 0:
  10.6 89.2 all-gather.2
  102.5 98.2 all-gather.4
  217.3 15.8 reduce-scatter.1
where the time goes:
time: 243 us; the launch traced here: 242 us
  waiting for transfers between devices  163 us (67%)
  local copies, waits for them, and re-layouts  42.7 us (18%)
  between operations  13.1 us (5%)
  matrix products  13 us (5%)
  other arithmetic  10.8 us (4%)
    all_gather x1, waiting for transfers between devices, on_device(): amp_slab = lax.all_gather(amplitudes, 'col', axis=1, tiled=True)  84.8 us
    all_gather x1, waiting for transfers between devices, on_device(): gathered = lax.all_gather(integrals, 'row', axis=0, tiled=True)  61.2 us
    gather x2, local copies, waits for them, and re-layouts, on_device(): jnp.take(amp_slab.reshape(mrow, slab_tiles, TS), local_ids, axis=1)  20.4 us
    reduce_scatter x1, waiting for transfers between devices, on_device(): lax.psum_scatter(partial_value, 'rep', scatter_dimension=1, tiled=True)  16 us
    dot_general x1, matrix products, on_device(): partial_value = jnp.dot(ordered, masked, preferred_element_type=jnp.float32)  13 us
    reshape x1, local copies, waits for them, and re-layouts, on_device(): amp_slab.reshape(mrow, slab_tiles, TS)  12 us
    select_n x1, other arithmetic, on_device(): jnp.take(amp_slab.reshape(mrow, slab_tiles, TS), local_ids, axis=1)  7.27 us
    unnamed x8, local copies, waits for them, and re-layouts  6.26 us
  transfers between devices with their start and end apart: 3, of which 3 were waited for; matrix products, arithmetic and copies ran while one was open for 18% of the time, Pallas kernels for 0%

commit v1 on v0

--- a/solution.py
+++ b/solution.py
@@ -23,7 +23,21 @@
     weights = jnp.logical_and(same, occupied).astype(jnp.bfloat16)
     shaped = gathered.reshape(slab_tiles, TS, tiles_col, TS) * weights[:, None, :, None]
     masked = shaped.reshape(kq, ncol)
-    amp_slab = lax.all_gather(amplitudes, "col", axis=1, tiled=True)
+    ways, here, step = (lax.axis_size("col"), lax.axis_index("col"), amplitudes.shape[1])
+    lengths = [n * ways if d == 1 else n for d, n in enumerate(amplitudes.shape)]
+    full = lax.dynamic_update_slice_in_dim(
+        jnp.zeros(lengths, amplitudes.dtype), amplitudes, here * step, axis=1
+    )
+    going_up = going_down = amplitudes
+    for far in range(1, ways // 2 + 1):
+        going_up = lax.ppermute(going_up, "col", [(d, (d + 1) % ways) for d in range(ways)])
+        full = lax.dynamic_update_slice_in_dim(full, going_up, (here - far) % ways * step, axis=1)
+        if 2 * far < ways:
+            going_down = lax.ppermute(going_down, "col", [(d, (d - 1) % ways) for d in range(ways)])
+            full = lax.dynamic_update_slice_in_dim(
+                full, going_down, (here + far) % ways * step, axis=1
+            )
+    amp_slab = full
     mrow = amp_slab.shape[0]
     local_ids = slots - slab * slab_tiles
     ordered = jnp.take(amp_slab.reshape(mrow, slab_tiles, TS), local_ids, axis=1).reshape(mrow, kq)

time: 243 us -> 196 us (0.81)
  waiting for transfers between devices: 163 us -> 95.9 us
  local copies, waits for them, and re-layouts: 42.7 us -> 56.3 us
  starting transfers between devices: 0.08 us -> 5.29 us
    all_gather x1 -> x0, waiting for transfers between devices: 84.8 us -> none  [on_device(): amp_slab = lax.all_gather(amplitudes, 'col', axis=1, tiled=True)]
    ppermute x0 -> x3, waiting for transfers between devices: none -> 72.4 us  [the longest x2 72.4 us: on_device(): lax.ppermute(going_up, 'col', [(d, (d + 1) % ways) for d in range(ways)])]
    all_gather x1, waiting for transfers between devices: 61.2 us -> 0.01 us  [on_device(): gathered = lax.all_gather(integrals, 'row', axis=0, tiled=True)]
    dynamic_update_slice x0 -> x4, local copies, waits for them, and re-layouts: none -> 10.8 us  [the longest x2 6.19 us: on_device(): lax.dynamic_update_slice_in_dim(full, going_up, (here - far) % ways * ste...]
    reduce_scatter x1, waiting for transfers between devices: 16 us -> 22.8 us  [on_device(): lax.psum_scatter(partial_value, 'rep', scatter_dimension=1, tiled=True)]
    ppermute x0 -> x3, starting transfers between devices: none -> 5.25 us  [the longest x2 3.72 us: on_device(): lax.ppermute(going_up, 'col', [(d, (d + 1) % ways) for d in range(ways)])]
    broadcast_in_dim x0 -> x1, local copies, waits for them, and re-layouts: none -> 4.38 us  [on_device(): jnp.zeros(lengths, amplitudes.dtype)]
  transfers between devices with their start and end apart: 3 -> 5, of which waited for: 3 -> 3; matrix products, arithmetic and copies ran while one was open for 18% -> 31% of each run, Pallas kernels for 0% -> 0%
where the time goes in v1:
time: 196 us; the launch traced here: 195 us
  waiting for transfers between devices  95.9 us (49%)
  local copies, waits for them, and re-layouts  56.3 us (29%)
  between operations  13.4 us (7%)
  matrix products  12.9 us (7%)
  other arithmetic  10.8 us (6%)
  starting transfers between devices  5.29 us (3%)
    ppermute x2, waiting for transfers between devices, on_device(): lax.ppermute(going_up, 'col', [(d, (d + 1) % ways) for d in range(ways)])  72.4 us
    reduce_scatter x1, waiting for transfers between devices, on_device(): lax.psum_scatter(partial_value, 'rep', scatter_dimension=1, tiled=True)  22.8 us
    gather x2, local copies, waits for them, and re-layouts, on_device(): jnp.take(amp_slab.reshape(mrow, slab_tiles, TS), local_ids, axis=1)  20.2 us
    dot_general x1, matrix products, on_device(): partial_value = jnp.dot(ordered, masked, preferred_element_type=jnp.float32)  12.9 us
    reshape x1, local copies, waits for them, and re-layouts, on_device(): amp_slab.reshape(mrow, slab_tiles, TS)  11.7 us
    select_n x1, other arithmetic, on_device(): jnp.take(amp_slab.reshape(mrow, slab_tiles, TS), local_ids, axis=1)  7.29 us
    dynamic_update_slice x2, local copies, waits for them, and re-layouts, on_device(): lax.dynamic_update_slice_in_dim(full, going_up, (here - far) % ways * ste...  6.19 us
    unnamed x8, local copies, waits for them, and re-layouts  5.19 us
  transfers between devices with their start and end apart: 5, of which 3 were waited for; matrix products, arithmetic and copies ran while one was open for 31% of the time, Pallas kernels for 0%

profile of v1, /device:TPU:1, one launch (start us, length us, event | category | flops | bytes accessed | tf_op | source)
XLA Modules:
  0.0 194.7 jit_solution(16962613610249732498)
XLA Ops:
  6.5 0.7 all-gather.2.cloned.1.call-update
  7.3 2.9 %copy.15 = bf16[1024,1024]{0,1:T(8,128)(2,1)S(1)} copy(bf16[1024,1024]{1,0:T(8,128)(2,1)} %param.6) | data formatting | bytes 4194304 | tf_op args[0]
  10.2 2.2 %collective-permute-start = (bf16[1024,1024]{0,1:T(8,128)(2,1)S(1)}, bf16[1024,1024]{0,1:T(8,128)(2,1)}, u32[]{:S(2)}, u32[]{:S(2)}) collective-permute-start(bf16[1024,1024]{0,1:T(8,128)(2,1)S(1)} %copy.15), channel_id=1, source_target_pairs={{0,2},{2,4},{4,6},{6,0},{1,3},{3,5},{5,7},{7,1},{8,10},{10,12},{12... | collective-permute-start | bytes 6291464 | tf_op jit(solution)/shard_map/ppermute | solution.py:33
  12.4 1.5 collective-permute-start.1
  13.9 43.4 %collective-permute-done = bf16[1024,1024]{0,1:T(8,128)(2,1)} collective-permute-done((bf16[1024,1024]{0,1:T(8,128)(2,1)S(1)}, bf16[1024,1024]{0,1:T(8,128)(2,1)}, u32[]{:S(2)}, u32[]{:S(2)}) %collective-permute-start) | collective-permute-done | bytes 2097184 | tf_op jit(solution)/shard_map/ppermute | solution.py:33
  57.3 1.5 collective-permute-start.2
  58.9 0.7 compare_and_fusion
  60.3 1.4 gather_fusion.1
  61.7 0.7 dynamic_slice.10
  62.6 4.4 %broadcast_in_dim.43 = bf16[1024,4096]{0,1:T(8,128)(2,1)} broadcast(bf16[]{:T(256)} %constant.77.clone.1), dimensions={} | broadcast | bytes 8388610 | tf_op jit(solution)/shard_map/broadcast_in_dim | solution.py:29
  67.0 1.5 constant_dynamic-update-slice_fusion.3
  68.5 3.1 %constant_dynamic-update-slice_fusion.2 = bf16[1024,4096]{0,1:T(8,128)(2,1)} fusion(bf16[1024,4096]{0,1:T(8,128)(2,1)} %constant_dynamic-update-slice_fusion.3, bf16[1024,1024]{0,1:T(8,128)(2,1)} %collective-permute-done, s32[]{:T(128)S(6)} %select_n.68), kind=kLoop, calls=%fused_computation.20 | loop fusion | bytes 4194308 | tf_op jit(solution)/shard_map/dynamic_update_slice | solution.py:34
  71.6 3.1 %constant_dynamic-update-slice_fusion.1 = bf16[1024,4096]{0,1:T(8,128)(2,1)} fusion(bf16[1024,4096]{0,1:T(8,128)(2,1)} %constant_dynamic-update-slice_fusion.2, bf16[1024,1024]{0,1:T(8,128)(2,1)} %collective-permute-done.1, s32[]{:T(128)S(6)} %select_n.70), kind=kLoop, calls=%fused_computation.19 | loop fusion | bytes 4194308 | tf_op jit(solution)/shard_map/dynamic_update_slice | solution.py:37
  74.7 29.0 %collective-permute-done.2 = bf16[1024,1024]{0,1:T(8,128)(2,1)} collective-permute-done((bf16[1024,1024]{0,1:T(8,128)(2,1)}, bf16[1024,1024]{0,1:T(8,128)(2,1)}, u32[]{:S(2)}, u32[]{:S(2)}) %collective-permute-start.2) | collective-permute-done | bytes 2097184 | tf_op jit(solution)/shard_map/ppermute | solution.py:33
  103.7 3.1 %constant_dynamic-update-slice_fusion = bf16[1024,4096]{0,1:T(8,128)(2,1)} fusion(bf16[1024,4096]{0,1:T(8,128)(2,1)} %constant_dynamic-update-slice_fusion.1, bf16[1024,1024]{0,1:T(8,128)(2,1)} %collective-permute-done.2, s32[]{:T(128)S(6)} %select_n.72), kind=kLoop, calls=%fused_computation.18 | loop fusion | bytes 4194308 | tf_op jit(solution)/shard_map/dynamic_update_slice | solution.py:34
  106.8 11.7 %copy.18 = bf16[1024,32,128]{2,0,1:T(8,128)(2,1)} copy(bf16[1024,32,128]{0,2,1:T(8,128)(2,1)} %bitcast.1) | data formatting | bytes 16777216 | tf_op jit(solution)/shard_map/reshape | solution.py:43
  118.5 8.4 %gather_fusion = bf16[32,1024,128]{2,1,0:T(8,128)(2,1)} fusion(bf16[1024,32,128]{2,0,1:T(8,128)(2,1)} %copy.18, s32[1024]{0:T(1024)S(1)} %get-tuple-element.12), kind=kCustom, calls=%fused_computation | custom fusion | bytes 16777344 | tf_op jit(solution)/shard_map/jit(_take)/gather | solution.py:43
  126.9 11.8 %copy.19 = bf16[1024,32,128]{0,2,1:T(8,128)(2,1)} copy(bf16[1024,32,128]{2,0,1:T(8,128)(2,1)} %bitcast.12) | data formatting | bytes 16777216 | tf_op jit(solution)/shard_map/jit(_take)/gather | solution.py:43
  138.7 7.3 %bitcast_select_fusion = bf16[1024,4096]{0,1:T(8,128)(2,1)} fusion(bf16[1024,32,128]{0,2,1:T(8,128)(2,1)} %copy.19, pred[4096]{0:T(1024)(128)(4,1)S(1)} %broadcast_bitcast_fusion), kind=kLoop, calls=%fused_computation.6 | loop fusion | flops 4194304 | bytes 16781312 | tf_op jit(solution)/shard_map/jit(_take)/select_n | solution.py:43
  146.0 1.1 mul.37
  147.2 2.2 %copy-done.2 = bf16[1024,4096]{0,1:T(8,128)(2,1)S(1)} copy-done((bf16[1024,4096]{0,1:T(8,128)(2,1)S(1)}, bf16[1024,4096]{0,1:T(8,128)(2,1)}, u32[]{:S(2)}) %copy-start.2) | copy-done | bytes 8388632
  149.4 12.9 %fusion = f32[1024,1024]{1,0:T(8,128)} fusion(bf16[1024,4096]{0,1:T(8,128)(2,1)S(1)} %copy-done.2, bf16[4096,1024]{1,0:T(8,128)(2,1)} %all-gather.2.cloned.1.call-done, bf16[512,8,8,128]{3,2,1,0:T(8,128)(2,1)S(1)} %bitcast.13), kind=kOutput, calls=%fused_computation.4 | convolution fusion | flops 8594128896 | bytes 29360128 | tf_op jit(solution)/shard_map/dot_general | solution.py:44
  162.3 22.8 %reduce-scatter.2.cloned.1.call-done = f32[1024,512]{1,0:T(8,128)} async-done(((f32[1024,1024]{1,0:T(8,128)}), f32[1024,512]{1,0:T(8,128)}) %reduce-scatter.2.cloned.1.call-update) | async-done | bytes 2097168 | tf_op jit(solution)/shard_map/reduce_scatter | solution.py:45
  185.1 2.7 %convert_element_type.11 = bf16[1024,512]{1,0:T(8,128)(2,1)} convert(f32[1024,512]{1,0:T(8,128)} %reduce-scatter.2.cloned.1.call-done) | non-fusion elementwise | flops 524288 | bytes 3145728 | tf_op jit(solution)/shard_map/convert_element_type | solution.py:45
  (19 shorter events, 1.0 us)
Async XLA Ops:
  6.5 52.3 %copy-start = (s32[64,32]{0,1:T(8,128)S(1)}, s32[64,32]{0,1:T(8,128)}, u32[]{:S(2)}) copy-start(s32[64,32]{0,1:T(8,128)} %param.8) | copy-start | bytes 24580
  6.5 139.5 %all-gather.2.cloned.1.call-start = ((), (), s32[]{:S(2)}) async-start(), calls=%async_computation.1 | async-start | bytes 8650752 | tf_op jit(solution)/shard_map/all_gather | solution.py:20
  7.3 177.9 %reduce-scatter.2.cloned.1.call-start = ((), (), s32[]{:S(2)}) async-start(), calls=%async_computation.2 | async-start | bytes 6291456 | tf_op jit(solution)/shard_map/reduce_scatter | solution.py:45
  10.2 47.1 %collective-permute-start = (bf16[1024,1024]{0,1:T(8,128)(2,1)S(1)}, bf16[1024,1024]{0,1:T(8,128)(2,1)}, u32[]{:S(2)}, u32[]{:S(2)}) collective-permute-start(bf16[1024,1024]{0,1:T(8,128)(2,1)S(1)} %copy.15), channel_id=1, source_target_pairs={{0,2},{2,4},{4,6},{6,0},{1,3},{3,5},{5,7},{7,1},{8,10},{10,12},{12... | collective-permute-start | bytes 6291464 | tf_op jit(solution)/shard_map/ppermute | solution.py:33
  12.4 59.3 %collective-permute-start.1 = (bf16[1024,1024]{0,1:T(8,128)(2,1)S(1)}, bf16[1024,1024]{0,1:T(8,128)(2,1)}, u32[]{:S(2)}, u32[]{:S(2)}) collective-permute-start(bf16[1024,1024]{0,1:T(8,128)(2,1)S(1)} %copy.15), channel_id=1, source_target_pairs={{0,6},{2,0},{4,2},{6,4},{1,7},{3,1},{5,3},{7,5},{8,14},{10,8},{12,... | collective-permute-start | bytes 6291464 | tf_op jit(solution)/shard_map/ppermute | solution.py:36
  57.3 46.4 %collective-permute-start.2 = (bf16[1024,1024]{0,1:T(8,128)(2,1)}, bf16[1024,1024]{0,1:T(8,128)(2,1)}, u32[]{:S(2)}, u32[]{:S(2)}) collective-permute-start(bf16[1024,1024]{0,1:T(8,128)(2,1)} %collective-permute-done), channel_id=1, source_target_pairs={{0,2},{2,4},{4,6},{6,0},{1,3},{3,5},{5,7},{7,1},{8,10},{10,12},{12... | collective-permute-start | bytes 6291464 | tf_op jit(solution)/shard_map/ppermute | solution.py:33
  146.0 3.4 %copy-start.2 = (bf16[1024,4096]{0,1:T(8,128)(2,1)S(1)}, bf16[1024,4096]{0,1:T(8,128)(2,1)}, u32[]{:S(2)}) copy-start(bf16[1024,4096]{0,1:T(8,128)(2,1)} %bitcast_select_fusion) | copy-start | bytes 25165828
  149.4 38.4 %copy-start.1 = (s32[64,32]{0,1:T(8,128)S(1)}, s32[64,32]{0,1:T(8,128)}, u32[]{:S(2)}) copy-start(s32[64,32]{0,1:T(8,128)} %param.8) | copy-start | bytes 24580
Sparse Core Ops, SparseCore 0:
  9.9 100.7 all-gather.1
  162.5 22.6 reduce-scatter.1
